TPU v7x, 256 devices: a whole 4x4x8 slice. The times are simulated.
256 devices in a mesh: row: 32 (over z, y_lo, core), col: 8 (over x, y_hi).
Axes of the slice: x: 4, y: 4 (y_hi: 2, y_lo: 2; y = y_hi * 2 + y_lo), z: 8, core: 2. Of those that a mesh axis runs over, the one named last changes fastest.
Arguments:
- activations: bfloat16 [1024, 16384], P('col', 'row'), may hold values from -6 to 6
- out_grad: bfloat16 [1024, 16384], P('col', 'row'), may hold values from -2 to 2
- gate_pre: bfloat16 [1024, 8192], P('row', 'col'), may hold values from -6 to 6
- up_pre: bfloat16 [1024, 8192], P('row', 'col'), may hold values from -6 to 6
- gate_weight: bfloat16 [16384, 8192], P('row', 'col'), may hold values from -0.046875 to 0.046875
- up_weight: bfloat16 [16384, 8192], P('row', 'col'), may hold values from -0.046875 to 0.046875
- down_weight: bfloat16 [8192, 16384], P('col', 'row'), may hold values from -0.0625 to 0.0625
Outputs:
- input_grad: bfloat16 [1024, 16384], P('col', 'row')
- gate_grad: bfloat16 [16384, 8192], P('row', 'col')
- up_grad: bfloat16 [16384, 8192], P('row', 'col')
- down_grad: bfloat16 [8192, 16384], P('col', 'row')
All inputs are finite; a program needn't handle non-finite values.
Results may differ from a plain program's by a relative error of at most 0.0051.
Values may be sent and summed in bfloat16 or wider, within the bound.
A program may use at most 64 MiB of HBM per device.

v0:
```python
import jax
import jax.numpy as jnp
from jax import lax
from jax.sharding import PartitionSpec as P


def contract_rows(left, right):
    return lax.dot_general(
        left, right, (((0,), (0,)), ((), ())), preferred_element_type=jnp.float32
    )


def contract_cols(left, right):
    return lax.dot_general(
        left, right, (((1,), (1,)), ((), ())), preferred_element_type=jnp.float32
    )


def derive(hidden_grad, gate_pre, up_pre):
    gate_val = gate_pre.astype(jnp.float32)
    up_val = up_pre.astype(jnp.float32)
    gate_sig = jax.nn.sigmoid(gate_val)
    swish_val = gate_val * gate_sig
    hidden = (swish_val * up_val).astype(jnp.bfloat16)
    gate_back = (hidden_grad * up_val * gate_sig * (1.0 + gate_val * (1.0 - gate_sig))).astype(
        jnp.bfloat16
    )
    up_back = (hidden_grad * swish_val).astype(jnp.bfloat16)
    return (hidden, gate_back, up_back)


def per_device(activations, out_grad, gate_pre, up_pre, gate_weight, up_weight, down_weight):
    acts_all, grad_all = (
        lax.all_gather(activations, "col", axis=0, tiled=True),
        lax.all_gather(out_grad, "col", axis=0, tiled=True),
    )
    grad_rows = grad_all
    hidden_grad = lax.psum_scatter(
        contract_cols(grad_rows, down_weight), "row", scatter_dimension=0, tiled=True
    )
    hidden, gate_back, up_back = derive(hidden_grad, gate_pre, up_pre)
    hid_piece = lax.all_gather(hidden, "row", axis=0, tiled=True)
    gate_piece = lax.all_gather(gate_back, "row", axis=0, tiled=True)
    up_piece = lax.all_gather(up_back, "row", axis=0, tiled=True)
    grad_rows = grad_all
    down_acc = contract_rows(hid_piece, grad_rows)
    gate_acc = contract_rows(acts_all, gate_piece)
    up_acc = contract_rows(acts_all, up_piece)
    input_rows = contract_cols(gate_piece, gate_weight) + contract_cols(up_piece, up_weight)
    input_acc = input_rows
    down_acc, gate_acc, up_acc, input_acc = (down_acc, gate_acc, up_acc, input_acc)
    input_grad = lax.psum_scatter(input_acc, "col", scatter_dimension=0, tiled=True)
    return (
        input_grad.astype(jnp.bfloat16),
        gate_acc.astype(jnp.bfloat16),
        up_acc.astype(jnp.bfloat16),
        down_acc.astype(jnp.bfloat16),
    )


def solution(mesh):
    placed = (
        P("col", "row"),
        P("col", "row"),
        P("row", "col"),
        P("row", "col"),
        P("row", "col"),
        P("row", "col"),
        P("col", "row"),
    )
    return jax.shard_map(
        per_device,
        mesh=mesh,
        in_specs=placed,
        out_specs=(P("col", "row"), P("row", "col"), P("row", "col"), P("col", "row")),
        check_vma=False,
    )
```

profile of v0, /device:TPU:32, one launch (start us, length us, event | category | flops | bytes accessed | tf_op | source)
XLA Modules:
  0.0 538.8 jit_solution(6172015009212809988)
XLA Ops:
  7.2 0.0 copy-start
  7.2 0.0 all-gather.6.cloned.1.call-start
  7.2 0.7 all-gather.6.cloned.1.call-update
  7.9 0.0 reduce-scatter.3.cloned.1.call-start
  8.0 57.5 %all-gather.6.cloned.1.call-done = bf16[1024,512]{1,0:T(8,128)(2,1)} async-done(((bf16[128,512]{1,0:T(8,128)(2,1)}), bf16[1024,512]{1,0:T(8,128)(2,1)}) %all-gather.6.cloned.1.call-update) | async-done | bytes 1048592 | tf_op jit(solution)/shard_map/all_gather | solution.py:35
  65.5 0.0 copy-done
  65.5 4.4 fusion.10
  69.9 0.0 copy-start.1
  69.9 0.0 copy-start.2
  70.0 0.0 copy-start.3
  70.0 0.0 reduce-scatter.3.cloned.1.call-update
  70.0 0.0 all-gather.8.cloned.1.call-start
  70.0 117.0 %reduce-scatter.3.cloned.1.call-done = f32[32,1024]{1,0:T(8,128)} async-done(((f32[1024,1024]{1,0:T(8,128)}), f32[32,1024]{1,0:T(8,128)}) %reduce-scatter.3.cloned.1.call-update) | async-done | bytes 131088 | tf_op jit(solution)/shard_map/reduce_scatter | solution.py:38
  187.1 0.0 copy-done.1
  187.1 0.0 copy-done.2
  187.1 1.6 multiply_convert_fusion
  188.7 0.0 all-gather.8.cloned.1.call-update
  188.7 0.0 all-gather.10.cloned.1.call-start
  188.8 0.5 all-gather.10.cloned.1.call-update
  189.3 0.0 all-gather.12.cloned.1.call-start
  189.4 0.5 all-gather.12.cloned.1.call-update
  189.9 0.0 all-gather.14.cloned.1.call-start
  189.9 0.5 all-gather.14.cloned.1.call-update
  190.5 0.0 copy-start.4
  190.5 0.0 reduce-scatter.5.cloned.1.call-start
  190.5 67.7 %all-gather.8.cloned.1.call-done = bf16[1024,1024]{1,0:T(8,128)(2,1)} async-done(((bf16[32,1024]{1,0:T(8,128)(2,1)}), bf16[1024,1024]{1,0:T(8,128)(2,1)}) %all-gather.8.cloned.1.call-update) | async-done | bytes 2097168 | tf_op jit(solution)/shard_map/all_gather | solution.py:43
  258.2 0.0 copy-done.3
  258.2 4.2 fusion.11
  262.5 62.1 %all-gather.10.cloned.1.call-done = bf16[1024,1024]{1,0:T(8,128)(2,1)} async-done(((bf16[32,1024]{1,0:T(8,128)(2,1)}), bf16[1024,1024]{1,0:T(8,128)(2,1)}) %all-gather.10.cloned.1.call-update) | async-done | bytes 2097168 | tf_op jit(solution)/shard_map/all_gather | solution.py:44
  324.5 0.0 copy-done.4
  324.5 4.9 convolution_add_fusion
  329.4 0.0 reduce-scatter.5.cloned.1.call-update
  329.5 50.4 %all-gather.12.cloned.1.call-done = bf16[1024,512]{1,0:T(8,128)(2,1)} async-done(((bf16[128,512]{1,0:T(8,128)(2,1)}), bf16[1024,512]{1,0:T(8,128)(2,1)}) %all-gather.12.cloned.1.call-update) | async-done | bytes 1048592 | tf_op jit(solution)/shard_map/all_gather | solution.py:34
  379.9 3.1 fusion
  383.0 0.0 copy-start.6
  383.0 1.3 copy.11
  384.3 0.0 copy-done.6
  384.3 2.9 fusion.1
  387.2 0.0 copy-start.5
  387.2 1.3 copy.12
  388.6 55.5 %all-gather.14.cloned.1.call-done = bf16[1024,1024]{1,0:T(8,128)(2,1)} async-done(((bf16[32,1024]{1,0:T(8,128)(2,1)}), bf16[1024,1024]{1,0:T(8,128)(2,1)}) %all-gather.14.cloned.1.call-update) | async-done | bytes 2097168 | tf_op jit(solution)/shard_map/all_gather | solution.py:42
  444.0 0.0 copy-done.5
  444.0 3.8 convolution_convert_fusion
  447.9 82.5 %reduce-scatter.5.cloned.1.call-done = f32[128,512]{1,0:T(8,128)} async-done(((f32[1024,512]{1,0:T(8,128)}), f32[128,512]{1,0:T(8,128)}) %reduce-scatter.5.cloned.1.call-update) | async-done | bytes 262160 | tf_op jit(solution)/shard_map/reduce_scatter | solution.py:52
  530.4 1.6 convert_element_type.37
Async XLA Ops:
  7.2 58.3 %copy-start = (bf16[1024,512]{1,0:T(8,128)(2,1)S(1)}, bf16[1024,512]{1,0:T(8,128)(2,1)}, u32[]{:S(2)}) copy-start(bf16[1024,512]{1,0:T(8,128)(2,1)} %param.13) | copy-start | bytes 3145732
  7.2 58.3 %all-gather.6.cloned.1.call-start = ((), (), s32[]{:S(2)}) async-start(), calls=%async_computation.2 | async-start | bytes 1179648 | tf_op jit(solution)/shard_map/all_gather | solution.py:35
  7.9 179.1 %reduce-scatter.3.cloned.1.call-start = ((), (), s32[]{:S(2)}) async-start(), calls=%async_computation.3 | async-start | bytes 4325376 | tf_op jit(solution)/shard_map/reduce_scatter | solution.py:38
  69.9 117.1 %copy-start.1 = (bf16[32,1024]{1,0:T(8,128)(2,1)S(1)}, bf16[32,1024]{1,0:T(8,128)(2,1)}, u32[]{:S(2)}) copy-start(bf16[32,1024]{1,0:T(8,128)(2,1)} %param.9) | copy-start | bytes 196612
  69.9 117.1 %copy-start.2 = (bf16[32,1024]{1,0:T(8,128)(2,1)S(1)}, bf16[32,1024]{1,0:T(8,128)(2,1)}, u32[]{:S(2)}) copy-start(bf16[32,1024]{1,0:T(8,128)(2,1)} %param.10) | copy-start | bytes 196612
  70.0 188.3 %copy-start.3 = (bf16[512,1024]{1,0:T(8,128)(2,1)S(1)}, bf16[512,1024]{1,0:T(8,128)(2,1)}, u32[]{:S(2)}) copy-start(bf16[512,1024]{1,0:T(8,128)(2,1)} %param.11) | copy-start | bytes 3145732
  70.0 188.2 %all-gather.8.cloned.1.call-start = ((), (), s32[]{:S(2)}) async-start(), calls=%async_computation.4 | async-start | bytes 2162688 | tf_op jit(solution)/shard_map/all_gather | solution.py:43
  188.7 135.8 %all-gather.10.cloned.1.call-start = ((), (), s32[]{:S(2)}) async-start(), calls=%async_computation.5 | async-start | bytes 2162688 | tf_op jit(solution)/shard_map/all_gather | solution.py:44
  189.3 190.6 %all-gather.12.cloned.1.call-start = ((), (), s32[]{:S(2)}) async-start(), calls=%async_computation.7 | async-start | bytes 1179648 | tf_op jit(solution)/shard_map/all_gather | solution.py:34
  189.9 254.2 %all-gather.14.cloned.1.call-start = ((), (), s32[]{:S(2)}) async-start(), calls=%async_computation.8 | async-start | bytes 2162688 | tf_op jit(solution)/shard_map/all_gather | solution.py:42
  190.5 134.1 %copy-start.4 = (bf16[512,1024]{1,0:T(8,128)(2,1)S(1)}, bf16[512,1024]{1,0:T(8,128)(2,1)}, u32[]{:S(2)}) copy-start(bf16[512,1024]{1,0:T(8,128)(2,1)} %param.12) | copy-start | bytes 3145732
  190.5 339.9 %reduce-scatter.5.cloned.1.call-start = ((), (), s32[]{:S(2)}) async-start(), calls=%async_computation.6 | async-start | bytes 2359296 | tf_op jit(solution)/shard_map/reduce_scatter | solution.py:52
  383.0 1.3 copy-start.6
  387.2 56.8 %copy-start.5 = (bf16[1024,512]{1,0:T(8,128)(2,1)S(1)}, bf16[1024,512]{1,0:T(8,128)(2,1)}, u32[]{:S(2)}) copy-start(bf16[1024,512]{1,0:T(8,128)(2,1)} %all-gather.6.cloned.1.call-done) | copy-start | bytes 3145732
Sparse Core Ops, SparseCore 0:
  10.6 54.8 all-gather.5
  70.1 116.9 reduce-scatter.2
  189.5 68.6 all-gather.7
  260.5 63.9 all-gather.9
  327.0 52.8 all-gather.11
  381.6 62.4 all-gather.13
  448.1 82.2 reduce-scatter.4
where the time goes:
time: 539 us
  waiting for transfers between devices  495 us (92%)
  matrix products  23.4 us (4%)
  between operations  14.2 us (3%)
    reduce_scatter x1, waiting for transfers between devices, per_device(): lax.psum_scatter(contract_cols(grad_rows, down_weight), 'row', scatter_di...  117 us
    reduce_scatter x1, waiting for transfers between devices, per_device(): lax.psum_scatter(input_acc, 'col', scatter_dimension=0, tiled=True)  82.5 us
    all_gather x1, waiting for transfers between devices, per_device(): gate_piece = lax.all_gather(gate_back, 'row', axis=0, tiled=True)  67.7 us
    all_gather x1, waiting for transfers between devices, per_device(): up_piece = lax.all_gather(up_back, 'row', axis=0, tiled=True)  62.1 us
    all_gather x1, waiting for transfers between devices, per_device(): lax.all_gather(out_grad, 'col', axis=0, tiled=True)  57.5 us
    all_gather x1, waiting for transfers between devices, per_device(): hid_piece = lax.all_gather(hidden, 'row', axis=0, tiled=True)  55.5 us
    all_gather x1, waiting for transfers between devices, per_device(): lax.all_gather(activations, 'col', axis=0, tiled=True)  50.4 us
    dot_general x3, matrix products, contract_cols(): lax.dot_general(left, right, (((1,), (1,)), ((), ())), preferred_element_...  13.6 us
  transfers between devices with their start and end apart: 7, of which 7 were waited for; matrix products, arithmetic and copies ran while one was open for 4% of the time, Pallas kernels for 0%

commit v1 on v0

--- a/solution.py
+++ b/solution.py
@@ -39,7 +39,8 @@
         contract_cols(grad_rows, down_weight), "row", scatter_dimension=0, tiled=True
     )
     hidden, gate_back, up_back = derive(hidden_grad, gate_pre, up_pre)
-    hid_piece = lax.all_gather(hidden, "row", axis=0, tiled=True)
+    outgoing = jnp.stack([hidden] * lax.axis_size("row"))
+    hid_piece = jnp.concatenate(lax.all_to_all(outgoing, "row", 0, 0), axis=0)
     gate_piece = lax.all_gather(gate_back, "row", axis=0, tiled=True)
     up_piece = lax.all_gather(up_back, "row", axis=0, tiled=True)
     grad_rows = grad_all

time: 539 us -> 488 us (0.905)
  waiting for transfers between devices: 495 us -> 426 us
  starting transfers between devices: 0.27 us -> 12.2 us
    all_gather x1 -> x0, waiting for transfers between devices: 55.5 us -> none  [per_device(): hid_piece = lax.all_gather(hidden, 'row', axis=0, tiled=True)]
    reduce_scatter x1, waiting for transfers between devices: 82.5 us -> 68.4 us  [per_device(): lax.psum_scatter(input_acc, 'col', scatter_dimension=0, tiled=True)]
    all_to_all x0 -> x1, starting transfers between devices: none -> 12 us  [per_device(): hid_piece = jnp.concatenate(lax.all_to_all(outgoing, 'row', 0, 0), axis=0)]
  transfers between devices with their start and end apart: 7 -> 7, of which waited for: 7 -> 6; matrix products, arithmetic and copies ran while one was open for 4% -> 6% of each run, Pallas kernels for 0% -> 0%
where the time goes in v1:
time: 488 us
  waiting for transfers between devices  426 us (87%)
  matrix products  25.9 us (5%)
  between operations  14.1 us (3%)
  starting transfers between devices  12.2 us (2%)
  local copies, waits for them, and re-layouts  6.17 us (1%)
    reduce_scatter x1, waiting for transfers between devices, per_device(): lax.psum_scatter(contract_cols(grad_rows, down_weight), 'row', scatter_di...  117 us
    all_gather x1, waiting for transfers between devices, per_device(): gate_piece = lax.all_gather(gate_back, 'row', axis=0, tiled=True)  69.3 us
    reduce_scatter x1, waiting for transfers between devices, per_device(): lax.psum_scatter(input_acc, 'col', scatter_dimension=0, tiled=True)  68.4 us
    all_gather x1, waiting for transfers between devices, per_device(): up_piece = lax.all_gather(up_back, 'row', axis=0, tiled=True)  62.1 us
    all_gather x1, waiting for transfers between devices, per_device(): lax.all_gather(out_grad, 'col', axis=0, tiled=True)  57.5 us
    all_gather x1, waiting for transfers between devices, per_device(): lax.all_gather(activations, 'col', axis=0, tiled=True)  50.1 us
    dot_general x3, matrix products, contract_cols(): lax.dot_general(left, right, (((1,), (1,)), ((), ())), preferred_element_...  14.2 us
    all_to_all x1, starting transfers between devices, per_device(): hid_piece = jnp.concatenate(lax.all_to_all(outgoing, 'row', 0, 0), axis=0)  12 us
  transfers between devices with their start and end apart: 7, of which 6 were waited for; matrix products, arithmetic and copies ran while one was open for 6% of the time, Pallas kernels for 0%

profile of v1, /device:TPU:32, one launch (start us, length us, event | category | flops | bytes accessed | tf_op | source)
XLA Modules:
  0.0 487.9 jit_solution(10217573537121033533)
XLA Ops:
  7.2 0.0 copy-start
  7.2 0.0 all-gather.5.cloned.1.call-start
  7.2 0.7 all-gather.5.cloned.1.call-update
  7.9 0.0 reduce-scatter.3.cloned.1.call-start
  8.0 57.5 %all-gather.5.cloned.1.call-done = bf16[1024,512]{1,0:T(8,128)(2,1)} async-done(((bf16[128,512]{1,0:T(8,128)(2,1)}), bf16[1024,512]{1,0:T(8,128)(2,1)}) %all-gather.5.cloned.1.call-update) | async-done | bytes 1048592 | tf_op jit(solution)/shard_map/all_gather | solution.py:35
  65.5 0.0 copy-done
  65.5 4.5 fusion.10
  70.0 0.0 copy-start.1
  70.0 0.0 copy-start.2
  70.0 0.0 reduce-scatter.3.cloned.1.call-update
  70.0 0.0 all-gather.7.cloned.1.call-start
  70.0 117.0 %reduce-scatter.3.cloned.1.call-done = f32[32,1024]{1,0:T(8,128)} async-done(((f32[1024,1024]{1,0:T(8,128)}), f32[32,1024]{1,0:T(8,128)}) %reduce-scatter.3.cloned.1.call-update) | async-done | bytes 131088 | tf_op jit(solution)/shard_map/reduce_scatter | solution.py:38
  187.1 0.0 copy-done.1
  187.1 0.0 copy-done.2
  187.1 1.6 multiply_convert_fusion
  188.7 0.0 all-gather.7.cloned.1.call-update
  188.7 0.0 all-gather.9.cloned.1.call-start
  188.8 0.5 all-gather.9.cloned.1.call-update
  189.3 0.0 all-gather.11.cloned.1.call-start
  189.4 0.5 all-gather.11.cloned.1.call-update
  189.9 1.6 stack.2
  191.5 12.0 %all-to-all-start = ((bf16[32,32,1024]{2,1,0:T(8,128)(2,1)}), bf16[32,32,1024]{2,1,0:T(8,128)(2,1)S(1)}, u32[]{:S(2)}, u32[]{:S(2)}) async-start(bf16[32,32,1024]{2,1,0:T(8,128)(2,1)} %stack.2), calls=%async_computation.2 | async-start | bytes 4194304 | tf_op jit(solution)/shard_map/all_to_all | solution.py:43
  203.5 0.0 reduce-scatter.5.cloned.1.call-start
  203.6 69.3 %all-gather.7.cloned.1.call-done = bf16[1024,1024]{1,0:T(8,128)(2,1)} async-done(((bf16[32,1024]{1,0:T(8,128)(2,1)}), bf16[1024,1024]{1,0:T(8,128)(2,1)}) %all-gather.7.cloned.1.call-update) | async-done | bytes 2097168 | tf_op jit(solution)/shard_map/all_gather | solution.py:44
  272.9 4.5 fusion.11
  277.4 62.1 %all-gather.9.cloned.1.call-done = bf16[1024,1024]{1,0:T(8,128)(2,1)} async-done(((bf16[32,1024]{1,0:T(8,128)(2,1)}), bf16[1024,1024]{1,0:T(8,128)(2,1)}) %all-gather.9.cloned.1.call-update) | async-done | bytes 2097168 | tf_op jit(solution)/shard_map/all_gather | solution.py:45
  339.5 5.2 %convolution_add_fusion = f32[1024,512]{1,0:T(8,128)} fusion(f32[1024,512]{1,0:T(8,128)} %fusion.11, bf16[1024,1024]{1,0:T(8,128)(2,1)} %all-gather.9.cloned.1.call-done, bf16[512,1024]{1,0:T(8,128)(2,1)} %param.12), kind=kOutput, calls=%fused_computation | convolution fusion | flops 1074266112 | bytes 7340032 | tf_op jit(solution)/shard_map/dot_general | solution.py:14
  344.7 0.0 reduce-scatter.5.cloned.1.call-update
  344.7 50.1 %all-gather.11.cloned.1.call-done = bf16[1024,512]{1,0:T(8,128)(2,1)} async-done(((bf16[128,512]{1,0:T(8,128)(2,1)}), bf16[1024,512]{1,0:T(8,128)(2,1)}) %all-gather.11.cloned.1.call-update) | async-done | bytes 1048592 | tf_op jit(solution)/shard_map/all_gather | solution.py:34
  394.8 4.1 fusion
  398.9 2.3 copy.11
  401.2 4.1 fusion.1
  405.3 2.3 copy.12
  407.5 0.0 all-to-all-done
  407.6 3.5 convolution_convert_fusion
  411.0 68.4 %reduce-scatter.5.cloned.1.call-done = f32[128,512]{1,0:T(8,128)} async-done(((f32[1024,512]{1,0:T(8,128)}), f32[128,512]{1,0:T(8,128)}) %reduce-scatter.5.cloned.1.call-update) | async-done | bytes 262160 | tf_op jit(solution)/shard_map/reduce_scatter | solution.py:53
  479.4 1.6 convert_element_type.37
Async XLA Ops:
  7.2 58.3 %copy-start = (bf16[1024,512]{1,0:T(8,128)(2,1)S(1)}, bf16[1024,512]{1,0:T(8,128)(2,1)}, u32[]{:S(2)}) copy-start(bf16[1024,512]{1,0:T(8,128)(2,1)} %param.13) | copy-start | bytes 3145732
  7.2 58.3 %all-gather.5.cloned.1.call-start = ((), (), s32[]{:S(2)}) async-start(), calls=%async_computation.3 | async-start | bytes 1179648 | tf_op jit(solution)/shard_map/all_gather | solution.py:35
  7.9 179.2 %reduce-scatter.3.cloned.1.call-start = ((), (), s32[]{:S(2)}) async-start(), calls=%async_computation.4 | async-start | bytes 4325376 | tf_op jit(solution)/shard_map/reduce_scatter | solution.py:38
  70.0 117.1 %copy-start.1 = (bf16[32,1024]{1,0:T(8,128)(2,1)S(1)}, bf16[32,1024]{1,0:T(8,128)(2,1)}, u32[]{:S(2)}) copy-start(bf16[32,1024]{1,0:T(8,128)(2,1)} %param.9) | copy-start | bytes 196612
  70.0 117.1 %copy-start.2 = (bf16[32,1024]{1,0:T(8,128)(2,1)S(1)}, bf16[32,1024]{1,0:T(8,128)(2,1)}, u32[]{:S(2)}) copy-start(bf16[32,1024]{1,0:T(8,128)(2,1)} %param.10) | copy-start | bytes 196612
  70.0 202.9 %all-gather.7.cloned.1.call-start = ((), (), s32[]{:S(2)}) async-start(), calls=%async_computation.5 | async-start | bytes 2162688 | tf_op jit(solution)/shard_map/all_gather | solution.py:44
  188.7 150.7 %all-gather.9.cloned.1.call-start = ((), (), s32[]{:S(2)}) async-start(), calls=%async_computation.6 | async-start | bytes 2162688 | tf_op jit(solution)/shard_map/all_gather | solution.py:45
  189.3 205.5 %all-gather.11.cloned.1.call-start = ((), (), s32[]{:S(2)}) async-start(), calls=%async_computation.8 | async-start | bytes 1179648 | tf_op jit(solution)/shard_map/all_gather | solution.py:34
  191.5 216.0 %all-to-all-start = ((bf16[32,32,1024]{2,1,0:T(8,128)(2,1)}), bf16[32,32,1024]{2,1,0:T(8,128)(2,1)S(1)}, u32[]{:S(2)}, u32[]{:S(2)}) async-start(bf16[32,32,1024]{2,1,0:T(8,128)(2,1)} %stack.2), calls=%async_computation.2 | async-start | bytes 4194304 | tf_op jit(solution)/shard_map/all_to_all | solution.py:43
  203.5 275.9 %reduce-scatter.5.cloned.1.call-start = ((), (), s32[]{:S(2)}) async-start(), calls=%async_computation.7 | async-start | bytes 2359296 | tf_op jit(solution)/shard_map/reduce_scatter | solution.py:53
Sparse Core Ops, SparseCore 0:
  10.6 54.8 all-gather.4
  70.1 116.9 reduce-scatter.2
  189.5 83.3 all-gather.6
  275.2 64.2 all-gather.8
  341.9 52.8 all-gather.10
  398.7 80.6 reduce-scatter.4
